TPU v7x, 32 devices: a whole 2x2x4 slice. The times are simulated.
32 devices in a mesh: chan: 8 (over z, y), facet: 4 (over x, core).
Axes of the slice: x: 2, y: 2, z: 4, core: 2. Of those that a mesh axis runs over, the one named last changes fastest.
Arguments:
- solution: float32 [8, 2048, 2048], P('chan', 'facet'), may hold values from -6 to 6
- residual: float32 [8, 2048, 2048], P('chan', 'facet'), may hold values from -120 to 120
- direction: float32 [8, 2048, 2048], P('chan', 'facet'), may hold values from -120 to 120
- spectra: float32 [8, 4096, 4096], P('chan', None, 'facet'), may hold values from 0.05 to 1
- basis: float32 [8, 8], replicated, may hold values from -2 to 2
- slot_channel: int32 [8], replicated, may hold values from 0 to 7, each once
Outputs:
- new_solution: float32 [8, 2048, 2048], P('chan', 'facet')
- new_residual: float32 [8, 2048, 2048], P('chan', 'facet')
- new_direction: float32 [8, 2048, 2048], P('chan', 'facet')
Inputs may be any that keep to these rules, and one draw needn't show every extreme that they name: `slot_channel`: every channel appears in exactly one slot.
All inputs are finite; a program needn't handle non-finite values.
Results may differ from a plain program's by a relative error of at most 0.000064.
Values sent between devices are 32-bit elements; how exact they have to be, the bound alone decides.
A program may use at most 256 MiB of HBM per device.

v0:
```python
import math

import jax
import jax.numpy as jnp
from jax import lax
from jax.sharding import PartitionSpec as P

ROOT = 64


HIGHEST = lax.Precision.HIGHEST
PRIOR_FLOOR = 0.25


def twiddle_table(left_size, right_size, length, direction_sign):
    product = (
        jnp.arange(left_size, dtype=jnp.int32)[:, None]
        * jnp.arange(right_size, dtype=jnp.int32)[None, :]
        % length
    )
    angles = product.astype(jnp.float32) * (2.0 * math.pi / length)
    return (jnp.cos(angles), direction_sign * jnp.sin(angles))


def complex_table(left_size, right_size, length, direction_sign):
    table_real, table_imag = twiddle_table(left_size, right_size, length, direction_sign)
    return jnp.stack([jnp.stack([table_real, table_imag]), jnp.stack([-table_imag, table_real])])


def real_table(left_size, right_size, length, direction_sign):
    table_real, table_imag = twiddle_table(left_size, right_size, length, direction_sign)
    return jnp.stack([table_real, table_imag])


def twisted(stacked, factor, direction_sign):
    table_real, table_imag = twiddle_table(factor, factor, factor * factor, direction_sign)
    table_real = table_real[:, :, None]
    table_imag = table_imag[:, :, None]
    real_in, imag_in = (stacked[0], stacked[1])
    return jnp.stack(
        [real_in * table_real - imag_in * table_imag, real_in * table_imag + imag_in * table_real]
    )


def forward_columns(planes, factor):
    halved = factor // 2
    groups, height = (planes.shape[0], planes.shape[1])
    blocks = planes.reshape(groups, height, halved, factor)
    section_one = jnp.einsum(
        "grjn,qjk->qgknr", blocks, real_table(halved, factor, factor, -1.0), precision=HIGHEST
    )
    section_one = twisted(section_one, factor, -1.0)
    second = jnp.einsum(
        "pgknr,pqnj->qgjkr",
        section_one,
        complex_table(factor, factor, factor, -1.0),
        precision=HIGHEST,
    )
    return second.reshape(2, groups, factor * factor, height)


def forward_rows(stacked, factor):
    halved = factor // 2
    groups, width = (stacked.shape[1], stacked.shape[2])
    blocks = stacked.reshape(2, groups, width, halved, factor)
    section_one = jnp.einsum(
        "pgcjn,pqjk->qgknc", blocks, complex_table(halved, factor, factor, -1.0), precision=HIGHEST
    )
    section_one = twisted(section_one, factor, -1.0)
    second = jnp.einsum(
        "pgknc,pqnj->qgjkc",
        section_one,
        complex_table(factor, factor, factor, -1.0),
        precision=HIGHEST,
    )
    return second.reshape(2, groups, factor * factor, width)


def inverse_rows(stacked, factor):
    halved = factor // 2
    groups, width = (stacked.shape[1], stacked.shape[3])
    blocks = stacked.reshape(2, groups, factor, factor, width)
    section_one = jnp.einsum(
        "pgjkc,pqjn->qgnkc", blocks, complex_table(factor, factor, factor, 1.0), precision=HIGHEST
    )
    section_one = twisted(section_one, factor, 1.0)
    second = jnp.einsum(
        "pgnkc,pqkj->qgjnc",
        section_one,
        complex_table(factor, halved, factor, 1.0),
        precision=HIGHEST,
    )
    return second.reshape(2, groups, halved * factor, width)


def inverse_columns(stacked, factor):
    halved = factor // 2
    groups, height = (stacked.shape[1], stacked.shape[2])
    blocks = stacked.reshape(2, groups, height, factor, factor)
    section_one = jnp.einsum(
        "pgrjk,pqjn->qgnkr", blocks, complex_table(factor, factor, factor, 1.0), precision=HIGHEST
    )
    section_one = twisted(section_one, factor, 1.0)
    table_real, table_imag = twiddle_table(factor, halved, factor, 1.0)
    last_table = jnp.stack([table_real, -table_imag])
    real_out = jnp.einsum("pgnkr,pkj->grjn", section_one, last_table, precision=HIGHEST)
    scaling = 1.0 / float(factor**4)
    return real_out.reshape(groups, height, halved * factor) * scaling


def body(solution, residual, direction, spectra, basis, slot_channel):
    channel_count = basis.shape[0]
    columns = forward_columns(direction, ROOT)
    swapped = lax.all_to_all(columns, "facet", split_axis=2, concat_axis=3, tiled=True)
    row_spectra = forward_rows(swapped, ROOT)
    weighted = row_spectra * spectra[None]
    inverted = inverse_rows(weighted, ROOT)
    returned = lax.all_to_all(inverted, "facet", split_axis=2, concat_axis=3, tiled=True)
    blurred = inverse_columns(returned, ROOT)
    regrouped = lax.all_to_all(direction, "chan", split_axis=2, concat_axis=0, tiled=True)
    one_hot = (slot_channel[:, None] == jnp.arange(channel_count, dtype=jnp.int32)[None, :]).astype(
        jnp.float32
    )
    loadings = jnp.dot(one_hot, basis, precision=HIGHEST)
    coeffs = jnp.einsum("cq,cij->qij", loadings, regrouped, precision=HIGHEST)
    local_prior = PRIOR_FLOOR * regrouped + jnp.einsum(
        "cq,qij->cij", loadings, coeffs, precision=HIGHEST
    )
    prior_term = lax.all_to_all(local_prior, "chan", split_axis=0, concat_axis=2, tiled=True)
    applied = blurred + prior_term
    norm_now, curvature = lax.psum(
        (jnp.sum(residual * residual), jnp.sum(direction * applied)), ("chan", "facet")
    )
    step_size = norm_now / curvature
    new_solution = solution + step_size * direction
    new_residual = residual - step_size * applied
    norm_next = lax.psum(jnp.sum(new_residual * new_residual), ("chan", "facet"))
    new_direction = new_residual + norm_next / norm_now * direction
    return (new_solution, new_residual, new_direction)


def solution(mesh):
    return jax.shard_map(
        body,
        mesh=mesh,
        in_specs=(
            P("chan", "facet", None),
            P("chan", "facet", None),
            P("chan", "facet", None),
            P("chan", None, "facet"),
            P(),
            P(),
        ),
        out_specs=(P("chan", "facet", None), P("chan", "facet", None), P("chan", "facet", None)),
        check_vma=False,
    )
```

profile of v0, /device:TPU:0, one launch (start us, length us, event | category | flops | bytes accessed | tf_op | source)
XLA Modules:
  0.0 1117.8 jit_solution(16000557213750763182)
XLA Ops:
  25.5 17.9 %convolution_bitcast_fusion.1 = f32[2,1,64,64,512]{4,2,3,0,1:T(8,128)S(1)} fusion(f32[512,32,64]{0,2,1:T(8,128)} %bitcast.178, f32[1,32,64]{2,1,0:T(8,128)S(1)} %get-tuple-element.34, f32[1,32,64]{2,1,0:T(8,128)S(1)} %get-tuple-element.35), kind=kOutput, calls=%fused_computation.36 | convolution fusion | flops 1610616832 | bytes 20987904 | tf_op jit(solution)/shard_map/grjn,qjk->qgknr/dot_general | solution.py:49
  62.4 43.8 %fusion.21 = f32[2,64,64,512]{3,1,2,0:T(8,128)} fusion(f32[2,64,64,512]{3,1,2,0:T(8,128)} %maximum_bitcast_fusion.2, f32[1,2,64,64]{2,3,0,1:T(8,128)S(1)} %get-tuple-element.27, f32[1,2,64,64]{2,3,0,1:T(8,128)S(1)} %get-tuple-element.28), kind=kOutput, calls=%fused_computation.33 | convolution fusion | flops 6442467328 | bytes 33619968 | tf_op jit(solution)/shard_map/pgknr,pqnj->qgjkr/dot_general | solution.py:53
  106.2 15.3 %copy.83 = f32[2,64,64,512]{3,2,1,0:T(8,128)S(1)} copy(f32[2,64,64,512]{3,1,2,0:T(8,128)} %fusion.21) | data formatting | bytes 33554432 | tf_op jit(solution)/shard_map/pgknr,pqnj->qgjkr/dot_general | solution.py:53
  121.5 32.2 %copy.84 = f32[2,1,4096,512]{3,0,1,2:T(2,128)} copy(f32[2,1,4096,512]{3,2,0,1:T(8,128)S(1)} %bitcast.181) | data formatting | bytes 33554432 | tf_op jit(solution)/shard_map/reshape;pgknr,pqnj->qgjkr/transpose | solution.py:59
  160.7 17.8 %copy.90 = f32[64,64,1024]{2,0,1:T(8,128)} copy(f32[64,64,1024]{2,1,0:T(8,128)} %bitcast.185) | data formatting | bytes 33554432 | tf_op jit(solution)/shard_map/mul | solution.py:116
  204.3 139.5 %all-to-all-done = f32[2,1,4096,512]{3,0,1,2:T(2,128)} async-done(((f32[2,1,4096,512]{3,0,1,2:T(2,128)}), f32[2,1,4096,512]{3,0,1,2:T(2,128)}, u32[]{:S(2)}, u32[]{:S(2)}) %all-to-all-start) | async-done | bytes 16777248 | tf_op jit(solution)/shard_map/all_to_all | solution.py:114
  364.3 16.5 %copy.86 = f32[2,1,1024,4,512]{2,4,3,0,1:T(8,128)} copy(f32[2,1,1024,4,512]{4,2,3,0,1:T(8,128)} %bitcast.182) | data formatting | bytes 33554432 | tf_op jit(solution)/shard_map/all_to_all | solution.py:114
  380.8 43.3 %convolution_bitcast_fusion = f32[2,1,64,64,1024]{4,2,3,0,1:T(8,128)} fusion(f32[2,1024,32,64]{1,3,2,0:T(8,128)} %bitcast.179, f32[1,2,32,64]{3,2,1,0:T(8,128)S(1)} %get-tuple-element.33, f32[1,2,32,64]{3,2,1,0:T(8,128)S(1)} %get-tuple-element.32), kind=kOutput, calls=%fused_computation.11 | convolution fusion | flops 6442459136 | bytes 50364416 | tf_op jit(solution)/shard_map/pgcjn,pqjk->qgknc/dot_general | solution.py:66
  424.1 17.6 %multiply_subtract_fusion = (f32[1,1,64,64,1024]{4,2,3,0,1:T(8,128)S(1)}, f32[1,1,64,64,1024]{4,2,3,0,1:T(8,128)}) fusion(f32[2,1,64,64,1024]{4,2,3,0,1:T(8,128)} %convolution_bitcast_fusion, f32[64,64]{0,1:T(8,128)S(1)} %get-tuple-element.36, f32[64,64]{0,1:T(8,128)S(1)} %get-tuple-element.37), kind=kLoop, calls=%fused_computation.28 | loop fusion | flops 25165824 | bytes 67141632 | tf_op jit(solution)/shard_map/sub | solution.py:41
  441.7 19.0 %maximum_bitcast_fusion = f32[2,64,64,1024,1]{3,1,2,0,4:T(8,128)} fusion(f32[1,1,64,64,1024]{4,2,3,0,1:T(8,128)} %get-tuple-element.19, f32[1,1,64,64,1024]{4,2,3,0,1:T(8,128)S(1)} %get-tuple-element.18), kind=kLoop, calls=%fused_computation | loop fusion | flops 8388608 | bytes 67108864 | tf_op jit(solution)/shard_map/reshape.24
  460.8 58.6 %fusion.4 = f32[2,64,64,1024,1]{3,1,4,0,2:T(8,128)} fusion(f32[2,64,64,1024,1]{3,1,2,0,4:T(8,128)} %maximum_bitcast_fusion, f32[1,2,64,64]{2,3,0,1:T(8,128)S(1)} %get-tuple-element.27, f32[1,2,64,64]{2,3,0,1:T(8,128)S(1)} %get-tuple-element.28), kind=kOutput, calls=%fused_computation.7 | convolution fusion | flops 12884918272 | bytes 67174400 | tf_op jit(solution)/shard_map/pgknc,pqnj->qgjkc/dot_general | solution.py:70
  519.3 38.5 %fusion.7 = f32[2,64,64,1024]{3,1,2,0:T(8,128)} fusion(f32[2,64,64,1024,1]{3,1,4,0,2:T(8,128)} %fusion.4, f32[64,64,1024]{2,0,1:T(8,128)} %copy.90, f32[1,2,64,64]{2,3,1,0:T(8,128)S(1)} %copy-done.6, f32[1,2,64,64]{2,3,1,0:T(8,128)S(1)} %copy-done.5), kind=kOutput, calls=%fused_computation.10 | convolution fusion | flops 12893306880 | bytes 83951616 | tf_op jit(solution)/shard_map/pgjkc,pqjn->qgnkc/dot_general | solution.py:83
  557.9 17.7 %subtract_bitcast_fusion = (f32[1,1,64,64,1024]{4,2,3,1,0:T(8,128)S(1)}, f32[1,1,64,64,1024]{4,2,3,1,0:T(8,128)}) fusion(f32[2,64,64,1024]{3,1,2,0:T(8,128)} %fusion.7, f32[64,64]{0,1:T(8,128)S(1)} %fusion.73, f32[64,64]{0,1:T(8,128)S(1)} %get-tuple-element.37), kind=kLoop, calls=%fused_computation.25 | loop fusion | flops 25165824 | bytes 67141632 | tf_op jit(solution)/shard_map/stack | solution.py:40
  575.5 18.8 %maximum_bitcast_fusion.1 = f32[2,64,64,1024]{3,1,2,0:T(8,128)} fusion(f32[1,1,64,64,1024]{4,2,3,1,0:T(8,128)} %get-tuple-element.17, f32[1,1,64,64,1024]{4,2,3,1,0:T(8,128)S(1)} %get-tuple-element.16), kind=kLoop, calls=%fused_computation.1 | loop fusion | flops 8388608 | bytes 67108864 | tf_op jit(solution)/shard_map/reshape.38
  594.3 51.4 %fusion.27 = f32[2,32,64,1024]{3,1,2,0:T(8,128)S(1)} fusion(f32[2,64,64,1024]{3,1,2,0:T(8,128)} %maximum_bitcast_fusion.1, f32[1,2,64,32]{2,3,0,1:T(8,128)S(1)} %copy-done.12, f32[1,2,64,32]{2,3,0,1:T(8,128)S(1)} %copy-done.11), kind=kOutput, calls=%fused_computation.35 | convolution fusion | flops 6442459136 | bytes 50364416 | tf_op jit(solution)/shard_map/pgnkc,pqkj->qgjnc/dot_general | solution.py:87
  645.8 19.4 %copy.93 = f32[2,32,64,1024]{3,2,1,0:T(8,128)} copy(f32[2,32,64,1024]{3,1,2,0:T(8,128)S(1)} %fusion.27) | data formatting | bytes 33554432 | tf_op jit(solution)/shard_map/pgnkc,pqkj->qgjnc/dot_general | solution.py:87
  665.2 28.6 %copy.94 = f32[2,1,2048,1024]{3,0,1,2:T(2,128)} copy(f32[2,1,2048,1024]{3,2,0,1:T(8,128)} %bitcast.183) | data formatting | bytes 33554432 | tf_op jit(solution)/shard_map/reshape;pgnkc,pqkj->qgjnc/transpose | solution.py:93
  715.4 168.4 %all-to-all-done.1 = f32[2,1,2048,1024]{3,0,1,2:T(2,128)} async-done(((f32[2,1,2048,1024]{3,0,1,2:T(2,128)}), f32[2,1,2048,1024]{3,0,1,2:T(2,128)}, u32[]{:S(2)}, u32[]{:S(2)}) %all-to-all-start.1) | async-done | bytes 16777248 | tf_op jit(solution)/shard_map/all_to_all | solution.py:118
  883.8 15.8 %copy.95 = f32[2,1,2048,1024]{3,2,0,1:T(8,128)} copy(f32[2,1,2048,1024]{3,0,1,2:T(2,128)} %all-to-all-done.1) | data formatting | bytes 33554432 | tf_op jit(solution)/shard_map/all_to_all | solution.py:118
  899.6 16.4 %copy.96 = f32[2,1,512,4,1024]{2,4,3,0,1:T(8,128)} copy(f32[2,1,512,4,1024]{4,2,3,0,1:T(8,128)} %bitcast.184) | data formatting | bytes 33554432 | tf_op jit(solution)/shard_map/all_to_all | solution.py:118
  916.1 33.0 %fusion.24 = f32[2,1,64,64,512]{4,2,3,0,1:T(8,128)} fusion(f32[2,512,64,64]{1,3,2,0:T(8,128)} %bitcast.180, f32[1,2,64,64]{2,3,1,0:T(8,128)S(1)} %copy-done.6, f32[1,2,64,64]{2,3,1,0:T(8,128)S(1)} %copy-done.5), kind=kOutput, calls=%fused_computation.34 | convolution fusion | flops 6442467328 | bytes 33619968 | tf_op jit(solution)/shard_map/pgrjk,pqjn->qgnkr/dot_general | solution.py:100
  967.5 18.7 %fusion.33 = f32[1,512,32,64]{1,2,3,0:T(8,128)S(1)} fusion(f32[2,64,64,512]{3,1,2,0:T(8,128)S(1)} %maximum_bitcast_fusion.3, f32[1,64,32]{1,2,0:T(8,128)S(1)} %copy-done.10, f32[1,64,32]{1,2,0:T(8,128)S(1)} %copy-done.8), kind=kOutput, calls=%fused_computation.43 | convolution fusion | flops 1611665408 | bytes 20987904 | tf_op jit(solution)/shard_map/pgnkr,pkj->grjn/dot_general | solution.py:106
  998.1 40.3 %all-reduce = (f32[]{:T(128)}, f32[]{:T(128)}) all-reduce(f32[]{:T(128)} %multiply_reduce_fusion.2, f32[]{:T(128)} %multiply_reduce_fusion.1), channel_id=1, replica_groups=mesh['chan'=8,'facet'=4] {'chan','facet'}, use_global_device_ids=true, to_apply=%region_1.2 | all-reduce | flops 2 | bytes 16 | tf_op jit(solution)/shard_map/psum | solution.py:131
  1048.9 41.4 %psum.23 = f32[]{:T(128)} all-reduce(f32[]{:T(128)} %get-tuple-element.14), channel_id=1, replica_groups=mesh['chan'=8,'facet'=4] {'chan','facet'}, use_global_device_ids=true, to_apply=%region_5.6 | all-reduce | flops 1 | bytes 8 | tf_op jit(solution)/shard_map/psum | solution.py:137
  (70 shorter events, 183.8 us)
Async XLA Ops:
  0.6 178.9 %copy-start = (f32[8,8]{1,0:T(8,128)S(1)}, f32[8,8]{1,0:T(8,128)}, u32[]{:S(2)}) copy-start(f32[8,8]{1,0:T(8,128)} %param.10) | copy-start | bytes 772
  11.5 142.2 %all-to-all-start.2 = ((f32[1,512,2048]{1,0,2:T(1,128)}), f32[1,512,2048]{1,0,2:T(1,128)}, u32[]{:S(2)}, u32[]{:S(2)}) async-start(f32[1,512,2048]{1,0,2:T(1,128)} %copy.101), calls=%async_computation.2 | async-start | bytes 8388608 | tf_op jit(solution)/shard_map/all_to_all | solution.py:120
  153.8 190.0 %all-to-all-start = ((f32[2,1,4096,512]{3,0,1,2:T(2,128)}), f32[2,1,4096,512]{3,0,1,2:T(2,128)}, u32[]{:S(2)}, u32[]{:S(2)}) async-start(f32[2,1,4096,512]{3,0,1,2:T(2,128)} %copy.84), calls=%async_computation | async-start | bytes 33554432 | tf_op jit(solution)/shard_map/all_to_all | solution.py:114
  160.7 18.8 %copy-start.13 = (s32[8]{0:T(128)S(1)}, s32[8]{0:T(128)}, u32[]{:S(2)}) copy-start(s32[8]{0:T(128)} %param.11) | copy-start | bytes 100
  178.7 22.3 %copy-start.7 = (f32[1,64,32]{1,2,0:T(8,128)}, f32[1,64,32]{1,2,0:T(8,128)S(1)}, u32[]{:S(2)}) copy-start(f32[1,64,32]{1,2,0:T(8,128)S(1)} %fusion.88) | copy-start | bytes 24580
  178.9 22.0 %copy-start.9 = (f32[1,64,32]{1,2,0:T(8,128)}, f32[1,64,32]{1,2,0:T(8,128)S(1)}, u32[]{:S(2)}) copy-start(f32[1,64,32]{1,2,0:T(8,128)S(1)} %get-tuple-element.43) | copy-start | bytes 24580
  343.8 350.0 %all-to-all-start.3 = ((f32[8,512,256]{2,1,0:T(8,128)}), f32[8,512,256]{2,1,0:T(8,128)}, u32[]{:S(2)}, u32[]{:S(2)}) async-start(f32[8,512,256]{2,1,0:T(8,128)} %copy.104), calls=%async_computation.3 | async-start | bytes 8388608 | tf_op jit(solution)/shard_map/all_to_all | solution.py:129
  460.8 58.6 %copy-start.5 = (f32[1,2,64,64]{2,3,1,0:T(8,128)S(1)}, f32[1,2,64,64]{2,3,1,0:T(8,128)}, u32[]{:S(2)}) copy-start(f32[1,2,64,64]{2,3,1,0:T(8,128)} %get-tuple-element.26) | copy-start | bytes 98308
  460.8 58.6 %copy-start.6 = (f32[1,2,64,64]{2,3,1,0:T(8,128)S(1)}, f32[1,2,64,64]{2,3,1,0:T(8,128)}, u32[]{:S(2)}) copy-start(f32[1,2,64,64]{2,3,1,0:T(8,128)} %get-tuple-element.29) | copy-start | bytes 98308
  575.5 18.8 %copy-start.11 = (f32[1,2,64,32]{2,3,0,1:T(8,128)S(1)}, f32[1,2,64,32]{2,3,0,1:T(8,128)}, u32[]{:S(2)}) copy-start(f32[1,2,64,32]{2,3,0,1:T(8,128)} %get-tuple-element.30) | copy-start | bytes 49156
  575.5 18.8 %copy-start.12 = (f32[1,2,64,32]{2,3,0,1:T(8,128)S(1)}, f32[1,2,64,32]{2,3,0,1:T(8,128)}, u32[]{:S(2)}) copy-start(f32[1,2,64,32]{2,3,0,1:T(8,128)} %get-tuple-element.31) | copy-start | bytes 49156
  693.8 190.0 %all-to-all-start.1 = ((f32[2,1,2048,1024]{3,0,1,2:T(2,128)}), f32[2,1,2048,1024]{3,0,1,2:T(2,128)}, u32[]{:S(2)}, u32[]{:S(2)}) async-start(f32[2,1,2048,1024]{3,0,1,2:T(2,128)} %copy.94), calls=%async_computation.1 | async-start | bytes 33554432 | tf_op jit(solution)/shard_map/all_to_all | solution.py:118
  960.0 7.4 copy-start.8
  960.0 7.4 copy-start.10
  967.4 23.2 %copy-start.2 = (f32[1,512,2048]{1,2,0:T(8,128)S(1)}, f32[1,512,2048]{1,2,0:T(8,128)}, u32[]{:S(2)}) copy-start(f32[1,512,2048]{1,2,0:T(8,128)} %copy.106) | copy-start | bytes 12582916
  967.5 23.2 %copy-start.3 = (f32[1,512,8,256]{1,3,2,0:T(8,128)S(1)}, f32[1,512,8,256]{1,3,2,0:T(8,128)}, u32[]{:S(2)}) copy-start(f32[1,512,8,256]{1,3,2,0:T(8,128)} %copy.105) | copy-start | bytes 12582916
  988.6 2.0 copy-start.4
  1091.7 25.7 %copy-start.1 = (f32[8,8]{1,0:T(8,128)S(1)}, f32[8,8]{1,0:T(8,128)}, u32[]{:S(2)}) copy-start(f32[8,8]{1,0:T(8,128)} %param.10) | copy-start | bytes 772
where the time goes:
time: 1130 us; the launch traced here: 1120 us
  matrix products  317 us (28%)
  waiting for transfers between devices  308 us (27%)
  local copies, waits for them, and re-layouts  242 us (21%)
  other arithmetic  138 us (12%)
  blocking collectives  81.7 us (7%)
  starting transfers between devices  27.7 us (2%)
    all_to_all x1, waiting for transfers between devices, body(): lax.all_to_all(inverted, 'facet', split_axis=2, concat_axis=3, tiled=True)  168 us
    all_to_all x1, waiting for transfers between devices, body(): lax.all_to_all(columns, 'facet', split_axis=2, concat_axis=3, tiled=True)  140 us
    dot_general x1, matrix products, forward_rows(): jnp.einsum('pgknc,pqnj->qgjkc', section_one, complex_table(factor, factor...  58.6 us
    another operation x4, other arithmetic  57.3 us
    dot_general x1, matrix products, inverse_rows(): jnp.einsum('pgnkc,pqkj->qgjnc', section_one, complex_table(factor, halved...  51.4 us
    unnamed x36, local copies, waits for them, and re-layouts  49.6 us
    dot_general x1, matrix products, forward_columns(): jnp.einsum('pgknr,pqnj->qgjkr', section_one, complex_table(factor, factor...  43.8 us
    dot_general x1, matrix products, forward_rows(): jnp.einsum('pgcjn,pqjk->qgknc', blocks, complex_table(halved, factor, fac...  43.3 us
  transfers between devices with their start and end apart: 4, of which 2 were waited for; matrix products, arithmetic and copies ran while one was open for 48% of the time, Pallas kernels for 0%

commit v1 on v0

v1 whole, which is shorter than its diff:
```python
import math

import jax
import jax.numpy as jnp
from jax import lax
from jax.sharding import PartitionSpec as P

ROOT = 64


HIGH = lax.Precision.HIGH
HIGHEST = lax.Precision.HIGHEST
PRIOR_FLOOR = 0.25


def wave(product, length, direction_sign):
    angles = (product % length).astype(jnp.float32) * (2.0 * math.pi / length)
    return (jnp.cos(angles), direction_sign * jnp.sin(angles))


def span(size):
    return jnp.arange(size, dtype=jnp.int32)


def swap_pairs(array, count, bit):
    pairs = [(place, place ^ bit) for place in range(count)]
    return lax.ppermute(array, "facet", pairs)


def column_table(width, columns, length, first_column):
    column = first_column + span(columns)[None, :]
    coarse = width // ROOT
    coarse_real, coarse_imag = wave(span(coarse)[:, None] * ROOT * column, length, -1.0)
    fine_real, fine_imag = wave(span(ROOT)[:, None] * column, length, -1.0)
    coarse_real, coarse_imag = (coarse_real[:, None], coarse_imag[:, None])
    fine_real, fine_imag = (fine_real[None], fine_imag[None])
    table_real = (coarse_real * fine_real - coarse_imag * fine_imag).reshape(width, columns)
    table_imag = (coarse_real * fine_imag + coarse_imag * fine_real).reshape(width, columns)
    return lax.optimization_barrier((table_real, table_imag))


def complex_stack(real, imag):
    return jnp.stack([jnp.stack([real, imag]), jnp.stack([-imag, real])])


def row_spectrum_pass(planes, spectrum, row_digits, factor):
    halved, columns = (row_digits.shape[0], planes.shape[2])
    blocks = planes.reshape(2, halved, factor, columns)
    first = complex_stack(*wave(row_digits[:, None] * span(factor)[None, :], factor, -1.0))
    section = jnp.einsum("pjnc,pqjk->kqnc", blocks, first, precision=HIGH)
    spread = span(factor)[:, None, None] * span(factor)[None, :, None] + (
        span(factor)[None, :, None] * span(factor)[None, None, :] * factor
    )
    second = complex_stack(*wave(spread, factor * factor, -1.0))
    freqs = jnp.einsum("kpnc,pqknj->kqjc", section, second, precision=HIGH)
    spectrum = spectrum.reshape(factor, factor, columns).transpose(1, 0, 2)
    weighted = freqs * spectrum[:, None]
    third = complex_stack(*wave(spread, factor * factor, 1.0))
    section = jnp.einsum("kpjc,pqknj->kqnc", weighted, third, precision=HIGH)
    last = complex_stack(*wave(row_digits[:, None] * span(factor)[None, :], factor, 1.0))
    rows = jnp.einsum("kpnc,pqjk->qjnc", section, last, precision=HIGH)
    return rows.reshape(2, halved * factor, columns)


def body(solution, residual, direction, spectra, basis, slot_channel):
    channel_count = basis.shape[0]
    factor = ROOT
    length = factor * factor
    facets = lax.axis_size("facet")
    place = lax.axis_index("facet")
    height, width = direction.shape[1:]
    columns = spectra.shape[2]
    own = direction[0]

    blocks = {0: own}
    bit = facets // 2
    while bit:
        blocks.update({key ^ bit: swap_pairs(blocks[key], facets, bit) for key in list(blocks)})
        bit //= 2
    table_real, table_imag = column_table(width, columns, length, place * columns)

    near = [blocks[key] for key in range(facets // 2)]
    far = [blocks[key] for key in range(facets // 2, facets)]
    near_rows = jnp.concatenate(near, axis=0)
    far_rows = jnp.concatenate(far, axis=0)
    planes = jnp.stack(
        [
            jnp.concatenate(
                [jnp.dot(part, table, precision=HIGH) for part in (near_rows, far_rows)], axis=0
            )
            for table in (table_real, table_imag)
        ]
    )
    digits = height // factor
    row_digits = ((place ^ span(facets))[:, None] * digits + span(digits)[None, :]).reshape(-1)
    rows = row_spectrum_pass(planes, spectra[0], row_digits, factor)

    def partial(part):
        wide = (((1,), (1,)), ((), ()))
        return lax.dot_general(part[0], table_real, wide, precision=HIGH) + lax.dot_general(
            part[1], table_imag, wide, precision=HIGH
        )

    sums = {}
    half = facets // 2
    for base in (half, 0):
        image = partial(rows[:, base * height : (base + half) * height])
        for key in range(half):
            sums[base + key] = image[key * height : (key + 1) * height]
    bit = 1
    while bit < facets:
        sums = {
            key: sums[key] + swap_pairs(sums[key | bit], facets, bit)
            for key in sorted(sums, reverse=True)
            if not key & bit
        }
        bit *= 2
    blurred = sums[0][None] * (1.0 / float(length * length))

    regrouped = lax.all_to_all(direction, "chan", split_axis=1, concat_axis=0, tiled=True)
    one_hot = (slot_channel[:, None] == span(channel_count)[None, :]).astype(jnp.float32)
    loadings = jnp.dot(one_hot, basis, precision=HIGHEST)
    coeffs = jnp.einsum("cq,cij->qij", loadings, regrouped, precision=HIGHEST)
    local_prior = PRIOR_FLOOR * regrouped + jnp.einsum(
        "cq,qij->cij", loadings, coeffs, precision=HIGHEST
    )
    prior_term = lax.all_to_all(local_prior, "chan", split_axis=0, concat_axis=1, tiled=True)
    applied = blurred + prior_term
    moments = jnp.stack(
        [
            jnp.sum(residual * residual),
            jnp.sum(direction * applied),
            jnp.sum(residual * applied),
            jnp.sum(applied * applied),
        ]
    )
    norm_now, curvature, cross, square = lax.psum(moments, ("chan", "facet"))
    step_size = norm_now / curvature
    new_solution = solution + step_size * direction
    new_residual = residual - step_size * applied
    norm_next = norm_now - 2.0 * step_size * cross + step_size * step_size * square
    new_direction = new_residual + norm_next / norm_now * direction
    return (new_solution, new_residual, new_direction)


def solution(mesh):
    return jax.shard_map(
        body,
        mesh=mesh,
        in_specs=(
            P("chan", "facet", None),
            P("chan", "facet", None),
            P("chan", "facet", None),
            P("chan", None, "facet"),
            P(),
            P(),
        ),
        out_specs=(P("chan", "facet", None), P("chan", "facet", None), P("chan", "facet", None)),
        check_vma=False,
    )
```

time: 1130 us -> 687 us (0.61)
  local copies, waits for them, and re-layouts: 242 us -> 90.7 us
  waiting for transfers between devices: 308 us -> 159 us
  other arithmetic: 138 us -> 69.8 us
  blocking collectives: 81.7 us -> 40.9 us
  matrix products: 317 us -> 299 us
    all_to_all x4 -> x2, waiting for transfers between devices: 308 us -> 46.5 us  [the longest x1 46.5 us: body(): lax.all_to_all(local_prior, 'chan', split_axis=0, concat_axis=1, tiled=True)]
    ppermute x0 -> x6, waiting for transfers between devices: none -> 112 us  [swap_pairs(): return lax.ppermute(array, 'facet', pairs)]
    all_to_all x6 -> x0, local copies, waits for them, and re-layouts: 73.6 us -> none  [the longest x2 32.2 us: body(): lax.all_to_all(inverted, 'facet', split_axis=2, concat_axis=3, tiled=True)]
    another operation x8 -> x4, other arithmetic: 76.3 us -> 14.1 us  [the longest x3 11.5 us: complex_stack(): return jnp.stack([jnp.stack([real, imag]), jnp.stack([-imag, real])])]
    transpose x2 -> x0, local copies, waits for them, and re-layouts: 60.8 us -> none  [the longest x1 32.2 us: forward_columns(): return second.reshape(2, groups, factor * factor, height)]
    psum x2 -> x1, blocking collectives: 81.7 us -> 40.9 us  [body(): norm_now, curvature, cross, square = lax.psum(moments, ('chan', 'facet'))]
    sub x3 -> x0, other arithmetic: 35.4 us -> none  [twisted(): real_in * table_real - imag_in * table_imag]
    another operation x0 -> x4, local copies, waits for them, and re-layouts: none -> 34.5 us  [the longest x1 17.8 us: row_spectrum_pass(): spectrum = spectrum.reshape(factor, factor, columns).transpose(1, 0, 2)]
  transfers between devices with their start and end apart: 4 -> 8, of which waited for: 2 -> 4; matrix products, arithmetic and copies ran while one was open for 48% -> 62% of each run, Pallas kernels for 0% -> 0%
where the time goes in v1:
time: 687 us; the launch traced here: 682 us
  matrix products  299 us (44%)
  waiting for transfers between devices  159 us (23%)
  local copies, waits for them, and re-layouts  90.7 us (13%)
  other arithmetic  69.8 us (10%)
  blocking collectives  40.9 us (6%)
  starting transfers between devices  17.2 us (3%)
    ppermute x6, waiting for transfers between devices, swap_pairs(): return lax.ppermute(array, 'facet', pairs)  112 us
    dot_general x4, matrix products, body(): jnp.dot(part, table, precision=HIGH)  68.4 us
    dot_general x1, matrix products, row_spectrum_pass(): freqs = jnp.einsum('kpnc,pqknj->kqjc', section, second, precision=HIGH)  47.3 us
    all_to_all x1, waiting for transfers between devices, body(): lax.all_to_all(local_prior, 'chan', split_axis=0, concat_axis=1, tiled=True)  46.5 us
    psum x1, blocking collectives, body(): norm_now, curvature, cross, square = lax.psum(moments, ('chan', 'facet'))  40.9 us
    dot_general x1, matrix products, row_spectrum_pass(): rows = jnp.einsum('kpnc,pqjk->qjnc', section, last, precision=HIGH)  40.1 us
    dot_general x2, matrix products, partial(): lax.dot_general(part[0], table_real, wide, precision=HIGH)  36 us
    dot_general x2, matrix products, partial(): lax.dot_general(part[1], table_imag, wide, precision=HIGH)  35.1 us
  transfers between devices with their start and end apart: 8, of which 4 were waited for; matrix products, arithmetic and copies ran while one was open for 62% of the time, Pallas kernels for 0%

profile of v1, /device:TPU:0, one launch (start us, length us, event | category | flops | bytes accessed | tf_op | source)
XLA Modules:
  0.0 682.2 jit_solution(11598784250257221795)
XLA Ops:
  3.7 8.5 %copy.27 = f32[1,512,2048]{2,0,1:T(1,128)} copy(f32[1,512,2048]{2,1,0:T(8,128)} %param.8) | data formatting | bytes 8388608 | tf_op args[2]
  27.4 67.2 %collective-permute-done.1 = f32[512,2048]{1,0:T(8,128)} collective-permute-done((f32[512,2048]{1,0:T(8,128)}, f32[512,2048]{1,0:T(8,128)}, u32[]{:S(2)}, u32[]{:S(2)}) %collective-permute-start.1) | collective-permute-done | bytes 4194336 | tf_op jit(solution)/shard_map/ppermute | solution.py:27
  94.7 17.8 %copy.73 = f32[64,64,1024]{2,0,1:T(8,128)} copy(f32[64,64,1024]{2,1,0:T(8,128)} %bitcast.135) | data formatting | bytes 33554432 | tf_op jit(solution)/shard_map/reshape;squeeze | solution.py:56
  112.4 9.1 %fusion.41 = (f32[1,64,64,64]{2,3,1,0:T(8,128)S(1)}, f32[1,64,64,64]{2,3,1,0:T(8,128)S(1)}, f32[1,64,64,64]{2,3,1,0:T(8,128)S(1)}, f32[1,64,64,64]{2,3,1,0:T(8,128)S(1)}, f32[1,64,64,64]{2,3,1,0:T(8,128)}) fusion(s32[64,64]{0,1:T(8,128)S(1)} %broadcast_multiply_fusion.1, s32[64,64]{1,0:T(8,128)S(1)} %copy.17), kind=kLoop, calls=%fused_computation.73 | loop fusion | flops 4456448 | bytes 5275648 | tf_op jit(solution)/shard_map/sin | solution.py:18
  138.1 18.5 %fusion.17 = f32[1024,1024]{1,0:T(8,128)} fusion(f32[2048,1024]{1,0:T(8,128)} %bitcast.142, f32[512,2048]{1,0:T(8,128)} %collective-permute-done, f32[512,2048]{1,0:T(8,128)S(1)} %bitcast.129), kind=kOutput, calls=%fused_computation.26 | convolution fusion | flops 12886999040 | bytes 20971520 | tf_op jit(solution)/shard_map/dot_general | solution.py:89
  156.6 14.4 %fusion.16 = f32[1024,1024]{1,0:T(8,128)S(1)} fusion(f32[2048,1024]{1,0:T(8,128)S(1)} %bitcast.152, f32[512,2048]{1,0:T(8,128)} %collective-permute-done, f32[512,2048]{1,0:T(8,128)S(1)} %bitcast.130), kind=kOutput, calls=%fused_computation.25 | convolution fusion | flops 12886999040 | bytes 20971520 | tf_op jit(solution)/shard_map/dot_general | solution.py:89
  175.7 17.8 %fusion.79 = f32[1024,1024]{1,0:T(8,128)} fusion(f32[1024,2048]{1,0:T(8,128)} %constant_dynamic-update-slice_fusion, f32[2048,1024]{1,0:T(8,128)S(1)} %bitcast.147), kind=kOutput, calls=%fused_computation.140 | convolution fusion | flops 12884901888 | bytes 20971520 | tf_op jit(solution)/shard_map/dot_general | solution.py:89
  193.6 17.6 %fusion.80 = f32[1024,1024]{1,0:T(8,128)} fusion(f32[1024,2048]{1,0:T(8,128)} %constant_dynamic-update-slice_fusion, f32[2048,1024]{1,0:T(8,128)S(1)} %bitcast.153), kind=kOutput, calls=%fused_computation.141 | convolution fusion | flops 12884901888 | bytes 20971520 | tf_op jit(solution)/shard_map/dot_general | solution.py:89
  215.5 8.1 %copy.19 = f32[1,32,64,1024]{3,1,0,2:T(8,128)} copy(f32[1,32,64,1024]{3,2,1,0:T(8,128)S(1)} %bitcast.133) | data formatting | bytes 16777216 | tf_op jit(solution)/shard_map/stack | solution.py:86
  226.9 8.1 %copy.20 = f32[1,32,64,1024]{3,1,0,2:T(8,128)} copy(f32[1,32,64,1024]{3,2,1,0:T(8,128)S(1)} %bitcast.134) | data formatting | bytes 16777216 | tf_op jit(solution)/shard_map/stack | solution.py:86
  235.4 27.6 %convolution_bitcast_fusion = f32[64,2,64,1024,1]{3,0,2,1,4:T(8,128)} fusion(f32[1,32,64,1024]{3,1,0,2:T(8,128)} %copy.20, f32[1,32,64,1024]{3,1,0,2:T(8,128)} %copy.19, f32[1,2,32,64]{3,2,0,1:T(8,128)S(1)} %get-tuple-element.26, f32[1,2,32,64]{3,2,0,1:T(8,128)S(1)} %get-tuple-element.27), kind=kOutput, calls=%fused_computation.9 | convolution fusion | flops 3225427968 | bytes 50364416 | tf_op jit(solution)/shard_map/pjnc,pqjk->kqnc/dot_general | solution.py:50
  263.0 47.3 %fusion.4 = f32[64,2,64,1024,1]{3,2,1,0,4:T(8,128)} fusion(f32[64,2,64,1024,1]{3,0,2,1,4:T(8,128)} %convolution_bitcast_fusion, f32[2,2,64,64,64]{3,4,2,1,0:T(8,128)} %get-tuple-element.43), kind=kOutput, calls=%fused_computation.5 | convolution fusion | flops 6442450944 | bytes 71303168 | tf_op jit(solution)/shard_map/kpnc,pqknj->kqjc/dot_general | solution.py:55
  310.3 31.7 %fusion.11 = f32[64,2,64,1024]{3,2,1,0:T(8,128)} fusion(f32[64,2,64,1024,1]{3,2,1,0,4:T(8,128)} %fusion.4, f32[64,64,1024]{2,1,0:T(8,128)} %bitcast.126, f32[2,2,64,64,64]{3,4,2,1,0:T(8,128)} %get-tuple-element.42), kind=kOutput, calls=%fused_computation.15 | convolution fusion | flops 6450839552 | bytes 88080384 | tf_op jit(solution)/shard_map/kpjc,pqknj->kqnc/dot_general | solution.py:59
  342.0 40.1 %fusion.18 = f32[2,32,64,1024]{3,1,2,0:T(8,128)S(1)} fusion(f32[64,2,64,1024]{3,2,1,0:T(8,128)} %fusion.11, f32[1,2,32,64]{3,2,1,0:T(8,128)S(1)} %get-tuple-element.28, f32[1,2,32,64]{3,2,1,0:T(8,128)S(1)} %get-tuple-element.25), kind=kOutput, calls=%fused_computation.27 | convolution fusion | flops 3221233664 | bytes 50364416 | tf_op jit(solution)/shard_map/kpnc,pqjk->qjnc/dot_general | solution.py:61
  382.2 19.4 %copy.26 = f32[2,32,64,1024]{3,2,1,0:T(8,128)} copy(f32[2,32,64,1024]{3,1,2,0:T(8,128)S(1)} %fusion.18) | data formatting | bytes 33554432 | tf_op jit(solution)/shard_map/kpnc,pqjk->qjnc/dot_general | solution.py:61
  401.6 16.8 %fusion.25 = f32[1024,2048]{1,0:T(8,128)S(1)} fusion(f32[2048,1024]{1,0:T(8,128)} %bitcast.148, f32[2,2048,1024]{2,1,0:T(8,128)} %bitcast.136), kind=kOutput, calls=%fused_computation.38 | convolution fusion | flops 12884901888 | bytes 20971520 | tf_op jit(solution)/shard_map/dot_general | solution.py:100
  418.4 18.0 %fusion.37 = f32[1024,2048]{1,0:T(8,128)S(1)} fusion(f32[1024,2048]{1,0:T(8,128)S(1)} %fusion.25, f32[2048,1024]{1,0:T(8,128)} %bitcast.143, f32[2,2048,1024]{2,1,0:T(8,128)} %bitcast.137), kind=kOutput, calls=%fused_computation.65 | convolution fusion | flops 12886999040 | bytes 29360128 | tf_op jit(solution)/shard_map/dot_general | solution.py:100
  468.8 18.3 %fusion.30 = f32[1024,2048]{1,0:T(8,128)} fusion(f32[2048,1024]{1,0:T(8,128)} %bitcast.149, f32[2,2048,1024]{2,1,0:T(8,128)} %bitcast.138), kind=kOutput, calls=%fused_computation.46 | convolution fusion | flops 12884901888 | bytes 20971520 | tf_op jit(solution)/shard_map/dot_general | solution.py:100
  487.2 18.1 %fusion.36 = f32[1024,2048]{1,0:T(8,128)S(1)} fusion(f32[1024,2048]{1,0:T(8,128)} %fusion.30, f32[2048,1024]{1,0:T(8,128)} %bitcast.144, f32[2,2048,1024]{2,1,0:T(8,128)} %bitcast.139), kind=kOutput, calls=%fused_computation.64 | convolution fusion | flops 12886999040 | bytes 29360128 | tf_op jit(solution)/shard_map/dot_general | solution.py:100
  515.8 46.5 %all-to-all-done.1 = f32[8,64,2048]{2,1,0:T(8,128)} async-done(((f32[8,64,2048]{2,1,0:T(8,128)}), f32[8,64,2048]{2,1,0:T(8,128)}, u32[]{:S(2)}, u32[]{:S(2)}) %all-to-all-start.1) | async-done | bytes 4194336 | tf_op jit(solution)/shard_map/all_to_all | solution.py:127
  562.3 44.5 %collective-permute-done.5 = f32[512,2048]{1,0:T(8,128)} collective-permute-done((f32[512,2048]{1,0:T(8,128)}, f32[512,2048]{1,0:T(8,128)}, u32[]{:S(2)}, u32[]{:S(2)}) %collective-permute-start.5) | collective-permute-done | bytes 4194336 | tf_op jit(solution)/shard_map/ppermute | solution.py:27
  606.8 10.3 %multiply_reduce_fusion.1 = (f32[]{:T(128)}, f32[]{:T(128)}, f32[]{:T(128)}, f32[512,2048]{1,0:T(8,128)S(1)}) fusion(f32[1,512,2048]{2,1,0:T(8,128)} %param.7, f32[1,512,2048]{2,1,0:T(8,128)} %param.8, f32[8,64,2048]{2,1,0:T(8,128)} %all-to-all-done.1, f32[512,2048]{1,0:T(8,128)} %collective-permute-done.5, f32[512,2048]{1,0:T(8,128)} %collective-permute-done.3, ...), kind=kLoop, calls=%fused_computation.58 | loop fusion | flops 10485757 | bytes 29360140 | tf_op jit(solution)/shard_map/reduce_sum | solution.py:131
  623.5 40.9 %psum.7 = f32[4]{0:T(128)S(1)} all-reduce(f32[4]{0:T(128)S(1)} %pad_maximum_fusion.15), channel_id=1, replica_groups=mesh['chan'=8,'facet'=4] {'chan','facet'}, use_global_device_ids=true, to_apply=%region_4.5 | all-reduce | flops 4 | bytes 32 | tf_op jit(solution)/shard_map/psum | solution.py:137
  669.1 12.8 %multiply_add_fusion.1 = (f32[1,512,2048]{2,1,0:T(8,128)}, f32[1,512,2048]{2,1,0:T(8,128)}, f32[1,512,2048]{2,1,0:T(8,128)}) fusion(f32[1,512,2048]{2,1,0:T(8,128)} %param.8, f32[]{:T(128)S(6)} %div.7, f32[1,512,2048]{2,1,0:T(8,128)} %param.7, f32[512,2048]{1,0:T(8,128)} %copy-done.2, f32[]{:T(128)S(6)} %div.6, f32[1,512,2048]{2,1,0:T(8,128)} %param.6), kind=kLoop, calls=%fused_computation.54 | loop fusion | flops 6291456 | bytes 29360136 | tf_op jit(solution)/shard_map/add | solution.py:142
  (70 shorter events, 96.9 us)
Async XLA Ops:
  0.6 440.7 %copy-start = (f32[8,8]{1,0:T(8,128)S(1)}, f32[8,8]{1,0:T(8,128)}, u32[]{:S(2)}) copy-start(f32[8,8]{1,0:T(8,128)} %param.10) | copy-start | bytes 772
  0.6 93.9 %collective-permute-start.1 = (f32[512,2048]{1,0:T(8,128)}, f32[512,2048]{1,0:T(8,128)}, u32[]{:S(2)}, u32[]{:S(2)}) collective-permute-start(f32[512,2048]{1,0:T(8,128)} %bitcast.127), channel_id=1, source_target_pairs={{0,2},{1,3},{2,0},{3,1},{4,6},{5,7},{6,4},{7,5},{8,10},{9,11},{10,... | collective-permute-start | bytes 12582920 | tf_op jit(solution)/shard_map/ppermute | solution.py:27
  3.7 134.4 %collective-permute-start = (f32[512,2048]{1,0:T(8,128)}, f32[512,2048]{1,0:T(8,128)}, u32[]{:S(2)}, u32[]{:S(2)}) collective-permute-start(f32[512,2048]{1,0:T(8,128)} %bitcast.128), channel_id=1, source_target_pairs={{0,1},{1,0},{2,3},{3,2},{4,5},{5,4},{6,7},{7,6},{8,9},{9,8},{10,11... | collective-permute-start | bytes 12582920 | tf_op jit(solution)/shard_map/ppermute | solution.py:27
  12.2 429.3 %all-to-all-start = ((f32[1,512,2048]{2,0,1:T(1,128)}), f32[1,512,2048]{2,0,1:T(1,128)}, u32[]{:S(2)}, u32[]{:S(2)}) async-start(f32[1,512,2048]{2,0,1:T(1,128)} %copy.27), calls=%async_computation | async-start | bytes 8388608 | tf_op jit(solution)/shard_map/all_to_all | solution.py:120
  94.6 76.5 %collective-permute-start.2 = (f32[512,2048]{1,0:T(8,128)}, f32[512,2048]{1,0:T(8,128)}, u32[]{:S(2)}, u32[]{:S(2)}) collective-permute-start(f32[512,2048]{1,0:T(8,128)} %collective-permute-done.1), channel_id=1, source_target_pairs={{0,1},{1,0},{2,3},{3,2},{4,5},{5,4},{6,7},{7,6},{8,9},{9,8},{10,11... | collective-permute-start | bytes 12582920 | tf_op jit(solution)/shard_map/ppermute | solution.py:27
  133.1 5.0 copy-start.1
  133.1 23.5 %slice-start.4 = ((s8[8388608]{0:T(1024)(128)(4,1)}), s8[4194304]{0:T(1024)(128)(4,1)S(1)}, s32[]{:S(2)}) async-start(s8[8388608]{0:T(1024)(128)(4,1)} %bitcast.150), calls=%async_computation.6 | async-start | bytes 8388608
  138.1 18.5 %slice-start.5 = ((s8[8388608]{0:T(1024)(128)(4,1)}), s8[4194304]{0:T(1024)(128)(4,1)S(1)}, s32[]{:S(2)}) async-start(s8[8388608]{0:T(1024)(128)(4,1)} %bitcast.150), calls=%async_computation.7 | async-start | bytes 8388608
  138.1 37.7 %slice-start.2 = ((s8[8388608]{0:T(1024)(128)(4,1)}), s8[4194304]{0:T(1024)(128)(4,1)S(1)}, s32[]{:S(2)}) async-start(s8[8388608]{0:T(1024)(128)(4,1)} %bitcast.145), calls=%async_computation.4 | async-start | bytes 8388608
  156.6 19.1 %slice-start.3 = ((s8[8388608]{0:T(1024)(128)(4,1)}), s8[4194304]{0:T(1024)(128)(4,1)S(1)}, s32[]{:S(2)}) async-start(s8[8388608]{0:T(1024)(128)(4,1)} %bitcast.145), calls=%async_computation.5 | async-start | bytes 8388608
  436.4 4.5 copy-start.3
  436.4 5.0 copy-start.5
  440.9 67.6 %collective-permute-start.4 = (f32[512,2048]{1,0:T(8,128)}, f32[512,2048]{1,0:T(8,128)}, u32[]{:S(2)}, u32[]{:S(2)}) collective-permute-start(f32[512,2048]{1,0:T(8,128)} %slice.45), channel_id=1, source_target_pairs={{0,1},{1,0},{2,3},{3,2},{4,5},{5,4},{6,7},{7,6},{8,9},{9,8},{10,11... | collective-permute-start | bytes 12582920 | tf_op jit(solution)/shard_map/ppermute | solution.py:27
  462.8 99.5 %all-to-all-start.1 = ((f32[8,64,2048]{2,1,0:T(8,128)}), f32[8,64,2048]{2,1,0:T(8,128)}, u32[]{:S(2)}, u32[]{:S(2)}) async-start(f32[8,64,2048]{2,1,0:T(8,128)} %copy.31), calls=%async_computation.1 | async-start | bytes 8388608 | tf_op jit(solution)/shard_map/all_to_all | solution.py:127
  468.8 39.7 %slice-start = ((s8[8388608]{0:T(1024)(128)(4,1)}), s8[4194304]{0:T(1024)(128)(4,1)S(1)}, s32[]{:S(2)}) async-start(s8[8388608]{0:T(1024)(128)(4,1)} %bitcast.140), calls=%async_computation.2 | async-start | bytes 8388608
  487.2 21.3 %slice-start.1 = ((s8[8388608]{0:T(1024)(128)(4,1)}), s8[4194304]{0:T(1024)(128)(4,1)S(1)}, s32[]{:S(2)}) async-start(s8[8388608]{0:T(1024)(128)(4,1)} %bitcast.140), calls=%async_computation.3 | async-start | bytes 8388608
  505.2 3.2 copy-start.4
  508.5 7.3 %collective-permute-start.3 = (f32[512,2048]{1,0:T(8,128)S(1)}, f32[512,2048]{1,0:T(8,128)}, u32[]{:S(2)}, u32[]{:S(2)}) collective-permute-start(f32[512,2048]{1,0:T(8,128)S(1)} %slice.41), channel_id=1, source_target_pairs={{0,1},{1,0},{2,3},{3,2},{4,5},{5,4},{6,7},{7,6},{8,9},{9,8},{10,11... | collective-permute-start | bytes 12582920 | tf_op jit(solution)/shard_map/ppermute | solution.py:27
  513.6 93.3 %collective-permute-start.5 = (f32[512,2048]{1,0:T(8,128)}, f32[512,2048]{1,0:T(8,128)}, u32[]{:S(2)}, u32[]{:S(2)}) collective-permute-start(f32[512,2048]{1,0:T(8,128)} %slice_add_fusion), channel_id=1, source_target_pairs={{0,2},{1,3},{2,0},{3,1},{4,6},{5,7},{6,4},{7,5},{8,10},{9,11},{10,... | collective-permute-start | bytes 12582920 | tf_op jit(solution)/shard_map/ppermute | solution.py:27
  617.2 2.0 copy-start.2
